TPU v7x, 128 devices: a whole 4x4x4 slice. The times are simulated.
128 devices in a mesh: dp: 32 (over z, y, core), section: 4 (over x).
Axes of the slice: x: 4, y: 4, z: 4, core: 2. Of those that a mesh axis runs over, the one named last changes fastest.
Arguments:
- real_in: bfloat16 [256, 144, 512], P('dp'), may hold values from -48 to 48
- fake_in: bfloat16 [256, 144, 512], P('dp'), may hold values from -48 to 48
- kernel_first: bfloat16 [5, 512, 1024], P(None, None, 'section'), may hold values from -0.15625 to 0.15625
- kernel_second: bfloat16 [5, 1024, 1024], P(None, None, 'section'), may hold values from -0.125 to 0.125
Outputs:
- layer_loss: float32 [2], replicated
- grad_first: float32 [512, 5, 1024], P('dp', None, 'section')
- grad_second: float32 [1024, 5, 1024], P('dp', None, 'section')
All inputs are finite; a program needn't handle non-finite values.
Results may differ from a plain program's by a relative error of at most 0.012.
The roundings to bfloat16 on the way count: a program that leaves them out, or rounds other values in their place, can miss the bound.
Values may be sent and summed in bfloat16 or wider, within the bound.
No kernel may reach another device: no remote copies, remote signals or barrier semaphores. Data moves between devices by JAX's collectives and lax.ppermute only.
A program may use at most 128 MiB of HBM per device.

v0:
```python
import jax
import jax.numpy as jnp
from jax import lax
from jax.sharding import Mesh
from jax.sharding import PartitionSpec as P

K = 5
DP = ("dp_0", "dp_1", "dp_2")
DP_SECTION = ("dp_0", "dp_1", "dp_2", "section")
smooth_width = 0.1
leak_slope = 0.1


def copy_for_each(x, axis):
    count = lax.axis_size(axis)
    return lax.all_to_all(jnp.broadcast_to(x[None], (count, *x.shape)), axis, 0, 0, tiled=True)


def in_order(blocks, dim):
    shape = list(blocks.shape[1:])
    shape[dim] *= blocks.shape[0]
    return jnp.moveaxis(blocks, 0, dim).reshape(shape)


def gathered_copies(x, axis, dim):
    blocks = copy_for_each(x, axis)
    return in_order(blocks, dim)


def one_axis_at_a_time(x, axes):
    for axis in axes:
        x = lax.psum(x, axis)
    return x


def in_blocks(x, dim, count):
    shape = x.shape
    blocks = x.reshape(*shape[:dim], count, shape[dim] // count, *shape[dim + 1 :])
    return jnp.moveaxis(blocks, dim, 0)


def sum_packed(arrays, axis, dims):
    count = lax.axis_size(axis)
    blocks = [in_blocks(a, dim, count) for a, dim in zip(arrays, dims)]
    lines = jnp.concatenate([b.reshape(count, -1) for b in blocks], axis=1)
    span = max(16, -(-lines.shape[1] // 1024) * 8)
    lines = jnp.pad(lines, ((0, 0), (0, span * 128 - lines.shape[1]))).reshape(-1, 128)
    vector, at, finished = (lax.psum_scatter(lines, axis, tiled=True).reshape(-1), 0, [])
    for b in blocks:
        part = b[0]
        finished.append(vector[at : at + part.size].reshape(part.shape))
        at += part.size
    return tuple(finished)


def conv_strided(values, kernel, frames):
    padded = jnp.pad(values, ((0, 0), (2, 2), (0, 0)))
    summed = jnp.zeros((values.shape[0] * frames, kernel.shape[2]), jnp.float32)
    for tap in range(kernel.shape[0]):
        window = padded[:, tap : tap + 3 * frames - 2 : 3].reshape(-1, values.shape[2])
        summed = summed + jnp.dot(window, kernel[tap], preferred_element_type=jnp.float32)
    return summed.reshape(values.shape[0], frames, -1)


def conv_forward(values, kernel):
    frames = values.shape[1]
    padded = jnp.pad(values, ((0, 0), (2, 2), (0, 0)))
    summed = jnp.zeros((values.shape[0] * frames, kernel.shape[2]), jnp.float32)
    for tap in range(kernel.shape[0]):
        window = padded[:, tap : tap + frames].reshape(-1, values.shape[2])
        summed = summed + jnp.dot(window, kernel[tap], preferred_element_type=jnp.float32)
    return summed.reshape(values.shape[0], frames, -1)


def conv_backward(delta, kernel):
    frames = delta.shape[1]
    padded = jnp.pad(delta, ((0, 0), (2, 2), (0, 0)))
    summed = jnp.zeros((delta.shape[0] * frames, kernel.shape[1]), jnp.float32)
    for tap in range(kernel.shape[0]):
        window = padded[:, 4 - tap : 4 - tap + frames].reshape(-1, delta.shape[2])
        summed = summed + lax.dot_general(
            window, kernel[tap], (((1,), (1,)), ((), ())), preferred_element_type=jnp.float32
        )
    return summed.reshape(delta.shape[0], frames, -1)


def weight_term(values, delta, amount, stride):
    frames = delta.shape[1]
    padded = jnp.pad(values, ((0, 0), (2, 2), (0, 0)))
    flat_delta = delta.reshape(-1, delta.shape[2])
    pieces = []
    for tap in range(K):
        window = padded[:, tap : tap + stride * (frames - 1) + 1 : stride].reshape(-1, amount)
        pieces.append(
            lax.dot_general(
                window, flat_delta, (((0,), (0,)), ((), ())), preferred_element_type=jnp.float32
            )
        )
    return jnp.stack(pieces, axis=1)


def activate(pre):
    return jnp.where(pre > 0, pre, leak_slope * pre).astype(jnp.bfloat16)


def local_grad(feature, normaliser):
    half = feature.shape[0] // 2
    difference = feature[:half].astype(jnp.float32) - feature[half:].astype(jnp.float32)
    slope = (
        difference / jnp.sqrt(difference * difference + smooth_width * smooth_width) / normaliser
    )
    return jnp.concatenate([slope, -slope], axis=0)


def smooth_total(feature):
    half = feature.shape[0] // 2
    difference = feature[:half].astype(jnp.float32) - feature[half:].astype(jnp.float32)
    return jnp.sum(jnp.sqrt(difference * difference + smooth_width * smooth_width) - smooth_width)


def shards(real_in, fake_in, kernel_first, kernel_second):
    replicas = lax.axis_size(DP)
    frames = real_in.shape[1] // 3
    in_width = real_in.shape[2]
    width = kernel_second.shape[1]
    normaliser = float(real_in.shape[0] * frames)
    count_all = float(real_in.shape[0] * replicas * frames * width)
    values = jnp.concatenate([real_in, fake_in], axis=0)
    first = activate(conv_strided(values, kernel_first, frames))
    partial_first = smooth_total(first)
    whole_first = gathered_copies(first, "section", 2)
    second = activate(conv_forward(whole_first, kernel_second))
    partial_second = smooth_total(second)
    total_first, total_second = (
        one_axis_at_a_time(partial_first, DP_SECTION),
        one_axis_at_a_time(partial_second, DP_SECTION),
    )
    layer_loss = jnp.stack([total_first, total_second]) / count_all
    delta_second = (local_grad(second, normaliser) * jnp.where(second > 0, 1.0, leak_slope)).astype(
        jnp.bfloat16
    )
    upstream_terms = conv_backward(delta_second, kernel_second)
    upstream = lax.psum_scatter(
        upstream_terms.astype(jnp.bfloat16), "section", scatter_dimension=2, tiled=True
    )
    delta_first = (
        (local_grad(first, normaliser) + upstream.astype(jnp.float32))
        * jnp.where(first > 0, 1.0, leak_slope)
    ).astype(jnp.bfloat16)
    term_first = weight_term(values, delta_first, in_width, 3)
    term_second = weight_term(whole_first, delta_second, width, 1)
    grad_first, grad_second = tuple(
        (
            part.astype(jnp.float32)
            for part in sum_packed(
                (term_first.astype(jnp.bfloat16), term_second.astype(jnp.bfloat16)), DP, (0, 0)
            )
        )
    )
    return (layer_loss, grad_first, grad_second)


def solution(mesh):
    finer = Mesh(
        mesh.devices.reshape(4, 4, 2, mesh.shape["section"]), ("dp_0", "dp_1", "dp_2", "section")
    )
    return jax.shard_map(
        shards,
        mesh=finer,
        in_specs=(
            P(DP, None, None),
            P(DP, None, None),
            P(None, None, "section"),
            P(None, None, "section"),
        ),
        out_specs=(P(), P(DP, None, "section"), P(DP, None, "section")),
        check_vma=False,
    )
```

profile of v0, /device:TPU:0, one launch (start us, length us, event | category | flops | bytes accessed | tf_op | source)
XLA Modules:
  0.0 208.0 jit_solution(5430325532296938739)
XLA Ops:
  7.2 2.6 %fusion.3 = bf16[16,148,512]{2,1,0:T(8,128)(2,1)S(1)} fusion(bf16[8,144,512]{2,1,0:T(8,128)(2,1)} %param.5, bf16[8,144,512]{2,1,0:T(8,128)(2,1)} %param.4), kind=kLoop, calls=%fused_computation.7 | loop fusion | flops 10911744 | bytes 4784128 | tf_op jit(solution)/shard_map/concatenate | solution.py:128
  9.9 3.4 %slice.116 = bf16[16,48,512]{2,1,0:T(8,128)(2,1)} slice(bf16[16,148,512]{2,1,0:T(8,128)(2,1)S(1)} %fusion.3), slice={[0:16:1], [3:145:3], [0:512:1]} | slice | bytes 1572864 | tf_op jit(solution)/shard_map/slice | solution.py:60
  13.2 3.2 %slice.114 = bf16[16,48,512]{2,1,0:T(8,128)(2,1)} slice(bf16[16,148,512]{2,1,0:T(8,128)(2,1)S(1)} %fusion.3), slice={[0:16:1], [2:144:3], [0:512:1]} | slice | bytes 1572864 | tf_op jit(solution)/shard_map/slice | solution.py:60
  16.5 3.3 %slice.112 = bf16[16,48,512]{2,1,0:T(8,128)(2,1)} slice(bf16[16,148,512]{2,1,0:T(8,128)(2,1)S(1)} %fusion.3), slice={[0:16:1], [1:143:3], [0:512:1]} | slice | bytes 1572864 | tf_op jit(solution)/shard_map/slice | solution.py:60
  19.7 1.2 slice.110
  20.9 3.5 %slice.118 = bf16[16,48,512]{2,1,0:T(8,128)(2,1)} slice(bf16[16,148,512]{2,1,0:T(8,128)(2,1)S(1)} %fusion.3), slice={[0:16:1], [4:146:3], [0:512:1]} | slice | bytes 1572864 | tf_op jit(solution)/shard_map/slice | solution.py:60
  24.4 1.5 fusion.68
  25.9 1.3 convolution_add_fusion.7
  27.2 0.4 convolution_add_fusion.6
  27.6 0.7 copy-done.9
  28.3 0.4 convolution_add_fusion.5
  28.8 0.4 convolution_add_fusion.4
  29.3 0.7 copy-done.6
  30.1 24.9 %all_to_all.5 = bf16[4,16,48,256]{3,2,1,0:T(8,128)(2,1)S(1)} all-to-all(bf16[4,16,48,256]{3,2,1,0:T(8,128)(2,1)S(1)} %broadcast_in_dim.16), channel_id=1, replica_groups=mesh['dp_0'=4,'dp_1'=4,'dp_2'=2,'section'=4] {'section'}, dimensions={0} | all-to-all | bytes 3145728 | tf_op jit(solution)/shard_map/all_to_all | solution.py:16
  55.0 1.2 copy.16
  56.8 1.5 pad_slice_fusion
  58.4 1.1 copy-done
  59.5 0.6 fusion.52
  60.1 0.6 convolution_add_fusion.3
  60.7 0.6 convolution_add_fusion.2
  61.3 0.6 convolution_add_fusion.1
  61.9 0.6 convolution_add_fusion
  62.5 0.8 fusion.76
  63.8 0.5 pad_slice_fusion.4
  64.4 0.6 fusion.44
  65.0 0.6 fusion.47
  65.6 0.6 fusion.41
  66.2 0.6 fusion.50
  66.8 2.0 add_convert_fusion
  69.1 2.9 %fusion.75 = (f32[8,48,256]{2,1,0:T(8,128)}, f32[8,48,256]{2,1,0:T(8,128)}, f32[]{:T(128)}) fusion(bf16[16,48,256]{2,1,0:T(8,128)(2,1)} %copy-done.6), kind=kLoop, calls=%fused_computation.123 | loop fusion | flops 983039 | bytes 1179652 | tf_op jit(solution)/shard_map/neg | solution.py:112
  72.0 0.6 fusion.17
  72.7 0.8 copy-done.5
  73.5 0.6 fusion.15
  74.1 0.8 copy-done.2
  74.9 0.6 fusion.9
  75.5 0.6 fusion.13
  76.2 0.6 fusion.11
  76.8 3.7 %copy.19 = bf16[1024,5,256]{2,1,0:T(8,128)(2,1)} copy(bf16[1024,5,256]{2,0,1:T(8,128)(2,1)S(1)} %fusion.11) | data formatting | bytes 5242880 | tf_op jit(solution)/shard_map/stack | solution.py:99
  80.5 4.7 %convert_element_type.93 = bf16[32,40960]{1,0:T(8,128)(2,1)S(1)} reshape(bf16[1024,5,256]{2,1,0:T(8,128)(2,1)} %copy.19) | data formatting | bytes 5242880 | tf_op jit(solution)/shard_map/convert_element_type | solution.py:156
  85.2 10.0 %reduce-scatter.3.cloned.1.call-done = bf16[16,48,256]{2,1,0:T(8,128)(2,1)} async-done(((bf16[16,48,1024]{2,1,0:T(8,128)(2,1)}), bf16[16,48,256]{2,1,0:T(8,128)(2,1)}) %reduce-scatter.3.cloned.1.call-update) | async-done | bytes 393232 | tf_op jit(solution)/shard_map/reduce_scatter | solution.py:143
  95.2 1.5 fusion.37
  96.7 0.4 fusion.32
  97.2 0.7 copy-done.16
  97.9 0.4 fusion.30
  98.3 0.7 copy-done.14
  99.0 0.4 fusion.28
  99.4 0.7 copy-done.10
  100.1 0.4 fusion.26
  100.5 0.7 copy-done.12
  101.3 0.4 fusion.24
  101.7 2.2 %copy.18 = bf16[512,5,256]{2,1,0:T(8,128)(2,1)} copy(bf16[512,5,256]{2,0,1:T(8,128)(2,1)S(1)} %fusion.24) | data formatting | bytes 2621440 | tf_op jit(solution)/shard_map/stack | solution.py:99
  103.8 3.5 %convert_element_type.92 = bf16[32,20480]{1,0:T(8,128)(2,1)} reshape(bf16[512,5,256]{2,1,0:T(8,128)(2,1)} %copy.18) | data formatting | bytes 2621440 | tf_op jit(solution)/shard_map/convert_element_type | solution.py:156
  107.4 3.4 %pad_maximum_fusion = bf16[32,61440]{1,0:T(8,128)(2,1)} fusion(bf16[32,40960]{1,0:T(8,128)(2,1)S(1)} %convert_element_type.93, bf16[32,20480]{1,0:T(8,128)(2,1)} %convert_element_type.92), kind=kLoop, calls=%fused_computation.5 | loop fusion | flops 7864320 | bytes 7864320 | tf_op jit(solution)/shard_map/concatenate | solution.py:45
  110.8 5.4 %reshape.124 = bf16[15360,128]{1,0:T(8,128)(2,1)} reshape(bf16[32,61440]{1,0:T(8,128)(2,1)} %pad_maximum_fusion) | data formatting | bytes 7864320 | tf_op jit(solution)/shard_map/reshape | solution.py:47
  116.2 11.3 %all-reduce.5 = (f32[]{:T(128)}, f32[]{:T(128)}) all-reduce(f32[]{:T(128)} %get-tuple-element.35, f32[]{:T(128)} %get-tuple-element.34), channel_id=1, replica_groups=mesh['dp_0'=4,'dp_1'=4,'dp_2'=2,'section'=4] {'dp_0'}, use_global_device_ids=true, to_apply=%region_6.7 | all-reduce | flops 2 | bytes 16 | tf_op jit(solution)/shard_map/psum | solution.py:32
  127.6 11.1 %all-reduce.4 = (f32[]{:T(128)}, f32[]{:T(128)}) all-reduce(f32[]{:T(128)} %get-tuple-element.16, f32[]{:T(128)} %get-tuple-element.17), channel_id=1, replica_groups=mesh['dp_0'=4,'dp_1'=4,'dp_2'=2,'section'=4] {'dp_1'}, use_global_device_ids=true, to_apply=%region_7.8 | all-reduce | flops 2 | bytes 16 | tf_op jit(solution)/shard_map/psum | solution.py:32
  138.7 3.1 %all-reduce.6 = (f32[]{:T(128)}, f32[]{:T(128)}) all-reduce(f32[]{:T(128)} %get-tuple-element.14, f32[]{:T(128)} %get-tuple-element.15), channel_id=1, replica_groups=mesh['dp_0'=4,'dp_1'=4,'dp_2'=2,'section'=4] {'dp_2'}, use_global_device_ids=true, to_apply=%region_8.9 | all-reduce | flops 2 | bytes 16 | tf_op jit(solution)/shard_map/psum | solution.py:32
  141.7 9.6 %all-reduce.3 = (f32[1]{0:T(128)}, f32[1]{0:T(128)}) all-reduce(f32[1]{0:T(128)} %bitcast.23, f32[1]{0:T(128)} %bitcast.11), channel_id=1, replica_groups=mesh['dp_0'=4,'dp_1'=4,'dp_2'=2,'section'=4] {'section'}, use_global_device_ids=true, to_apply=%region_9.10 | all-reduce | flops 2 | bytes 16 | tf_op jit(solution)/shard_map/psum | solution.py:32
  151.4 1.9 maximum_multiply_fusion
  153.3 44.7 %reduce-scatter.5.cloned.1.call-done = bf16[480,128]{1,0:T(8,128)(2,1)} async-done(((bf16[15360,128]{1,0:T(8,128)(2,1)}), bf16[480,128]{1,0:T(8,128)(2,1)}) %reduce-scatter.5.cloned.1.call-update) | async-done | bytes 122896 | tf_op jit(solution)/shard_map/reduce_scatter | solution.py:48
  198.0 0.8 slice_convert_fusion.1
  198.8 0.7 copy.20
  199.5 0.9 slice_convert_fusion
  200.4 0.7 copy.21
  (48 shorter events, 1.9 us)
Async XLA Ops:
  7.2 88.0 %reduce-scatter.3.cloned.1.call-start = ((), (), s32[]{:S(2)}) async-start(), calls=%async_computation.3 | async-start | bytes 1966080 | tf_op jit(solution)/shard_map/reduce_scatter | solution.py:143
  20.9 6.3 %copy-start.7 = (bf16[16,48,512]{2,1,0:T(8,128)(2,1)}, bf16[16,48,512]{2,1,0:T(8,128)(2,1)S(1)}, u32[]{:S(2)}) copy-start(bf16[16,48,512]{2,1,0:T(8,128)(2,1)S(1)} %slice.110) | copy-start | bytes 2359300
  24.4 1.5 copy-start.15
  24.4 2.8 %copy-start.13 = (bf16[16,48,512]{2,1,0:T(8,128)(2,1)S(1)}, bf16[16,48,512]{2,1,0:T(8,128)(2,1)}, u32[]{:S(2)}) copy-start(bf16[16,48,512]{2,1,0:T(8,128)(2,1)} %slice.114) | copy-start | bytes 2359300
  24.4 2.8 %copy-start.21 = (bf16[5,512,256]{2,1,0:T(8,128)(2,1)S(1)}, bf16[5,512,256]{2,1,0:T(8,128)(2,1)}, u32[]{:S(2)}) copy-start(bf16[5,512,256]{2,1,0:T(8,128)(2,1)} %param.6) | copy-start | bytes 3932164
  27.2 1.1 copy-start.9
  27.6 1.2 copy-start.11
  29.3 0.8 copy-start.6
  56.6 4.1 %copy-start.1 = (bf16[96,8,4,256]{3,1,2,0:T(8,128)(2,1)}, bf16[96,8,4,256]{3,1,2,0:T(8,128)(2,1)S(1)}, u32[]{:S(2)}) copy-start(bf16[96,8,4,256]{3,1,2,0:T(8,128)(2,1)S(1)} %copy.23) | copy-start | bytes 4718596
  56.8 1.6 copy-start.3
  56.8 2.7 %copy-start = (bf16[5,1024,256]{2,1,0:T(8,128)(2,1)S(1)}, bf16[5,1024,256]{2,1,0:T(8,128)(2,1)}, u32[]{:S(2)}) copy-start(bf16[5,1024,256]{2,1,0:T(8,128)(2,1)} %param.7) | copy-start | bytes 7864324
  63.6 0.8 copy-start.17
  63.8 1.2 copy-start.19
  68.8 3.2 %copy-start.4 = (bf16[4,16,6,8,256]{4,3,0,2,1:T(8,128)(2,1)S(1)}, bf16[4,16,6,8,256]{4,3,0,2,1:T(8,128)(2,1)}, u32[]{:S(2)}) copy-start(bf16[4,16,6,8,256]{4,3,0,2,1:T(8,128)(2,1)} %copy-done.3) | copy-start | bytes 4718596
  68.8 3.2 %copy-start.18 = (bf16[16,48,256]{2,1,0:T(8,128)(2,1)S(1)}, bf16[16,48,256]{2,1,0:T(8,128)(2,1)}, u32[]{:S(2)}) copy-start(bf16[16,48,256]{2,1,0:T(8,128)(2,1)} %copy-done.17) | copy-start | bytes 1179652
  68.9 129.1 %reduce-scatter.5.cloned.1.call-start = ((), (), s32[]{:S(2)}) async-start(), calls=%async_computation.4 | async-start | bytes 4055040 | tf_op jit(solution)/shard_map/reduce_scatter | solution.py:48
  72.0 1.4 copy-start.5
  73.5 1.4 copy-start.2
  73.5 1.5 copy-start.20
  95.2 1.5 copy-start.8
  96.7 1.1 copy-start.16
  97.9 1.1 copy-start.14
  99.0 1.1 copy-start.10
  100.1 1.1 copy-start.12
Sparse Core Ops, SparseCore 0:
  69.0 26.1 reduce-scatter.2
  116.3 81.5 reduce-scatter.4
where the time goes:
time: 209 us; the launch traced here: 208 us
  blocking collectives  60 us (29%)
  waiting for transfers between devices  54.7 us (26%)
  local copies, waits for them, and re-layouts  46.6 us (22%)
  matrix products  16.4 us (8%)
  other arithmetic  15.4 us (7%)
  between operations  14.5 us (7%)
    reduce_scatter x1, waiting for transfers between devices, sum_packed(): lax.psum_scatter(lines, axis, tiled=True).reshape(-1)  44.7 us
    psum x4, blocking collectives, one_axis_at_a_time(): x = lax.psum(x, axis)  35.2 us
    all_to_all x1, blocking collectives, copy_for_each(): lax.all_to_all(jnp.broadcast_to(x[None], (count, *x.shape)), axis, 0, 0,...  24.9 us
    slice x5, local copies, waits for them, and re-layouts, conv_strided(): window = padded[:, tap:tap + 3 * frames - 2:3].reshape(-1, values.shape[2])  14.5 us
    reduce_scatter x1, waiting for transfers between devices, shards(): lax.psum_scatter(upstream_terms.astype(jnp.bfloat16), 'section', scatter_...  9.96 us
    unnamed x47, local copies, waits for them, and re-layouts  8.98 us
    another operation x2, local copies, waits for them, and re-layouts, weight_term(): return jnp.stack(pieces, axis=1)  5.81 us
    reshape x1, local copies, waits for them, and re-layouts, sum_packed(): jnp.pad(lines, ((0, 0), (0, span * 128 - lines.shape[1]))).reshape(-1, 128)  5.43 us
  transfers between devices with their start and end apart: 2, of which 2 were waited for; matrix products, arithmetic and copies ran while one was open for 8% of the time, Pallas kernels for 0%

commit v1 on v0

--- a/solution.py
+++ b/solution.py
@@ -29,7 +29,7 @@
 
 def one_axis_at_a_time(x, axes):
     for axis in axes:
-        x = lax.psum(x, axis)
+        x = jnp.sum(lax.all_gather(x, axis), axis=0)
     return x
 
 

time: 209 us -> 208 us (level)
  waiting for transfers between devices: 54.7 us -> 39.7 us
  local copies, waits for them, and re-layouts: 46.6 us -> 58 us
  other arithmetic: 15.4 us -> 19.1 us
  blocking collectives: 60 us -> 57.4 us
    psum x4 -> x0, blocking collectives: 35.2 us -> none  [one_axis_at_a_time(): x = lax.psum(x, axis)]
    unnamed x0 -> x4, blocking collectives: none -> 32.5 us
    reduce_scatter x1, waiting for transfers between devices: 44.7 us -> 28.3 us  [sum_packed(): lax.psum_scatter(lines, axis, tiled=True).reshape(-1)]
    unnamed x47 -> x59, local copies, waits for them, and re-layouts: 8.98 us -> 20.6 us
    reduce_sum x0 -> x8, other arithmetic: none -> 4.81 us  [one_axis_at_a_time(): x = jnp.sum(lax.all_gather(x, axis), axis=0)]
  transfers between devices with their start and end apart: 2 -> 2, of which waited for: 2 -> 2; matrix products, arithmetic and copies ran while one was open for 8% -> 17% of each run, Pallas kernels for 0% -> 0%
where the time goes in v1:
time: 208 us; the launch traced here: 207 us
  local copies, waits for them, and re-layouts  58 us (28%)
  blocking collectives  57.4 us (28%)
  waiting for transfers between devices  39.7 us (19%)
  other arithmetic  19.1 us (9%)
  matrix products  18 us (9%)
  between operations  14.4 us (7%)
    unnamed x4, blocking collectives  32.5 us
    reduce_scatter x1, waiting for transfers between devices, sum_packed(): lax.psum_scatter(lines, axis, tiled=True).reshape(-1)  28.3 us
    all_to_all x1, blocking collectives, copy_for_each(): lax.all_to_all(jnp.broadcast_to(x[None], (count, *x.shape)), axis, 0, 0,...  24.9 us
    unnamed x59, local copies, waits for them, and re-layouts  20.6 us
    slice x5, local copies, waits for them, and re-layouts, conv_strided(): window = padded[:, tap:tap + 3 * frames - 2:3].reshape(-1, values.shape[2])  14.5 us
    reduce_scatter x1, waiting for transfers between devices, shards(): lax.psum_scatter(upstream_terms.astype(jnp.bfloat16), 'section', scatter_...  11.3 us
    dot_general x10, matrix products, weight_term(): lax.dot_general(window, flat_delta, (((0,), (0,)), ((), ())), preferred_e...  6.75 us
    another operation x2, local copies, waits for them, and re-layouts, weight_term(): return jnp.stack(pieces, axis=1)  5.81 us
  transfers between devices with their start and end apart: 2, of which 2 were waited for; matrix products, arithmetic and copies ran while one was open for 17% of the time, Pallas kernels for 0%

profile of v1, /device:TPU:0, one launch (start us, length us, event | category | flops | bytes accessed | tf_op | source)
XLA Modules:
  0.0 206.9 jit_solution(15537374317017595011)
XLA Ops:
  7.2 2.6 %fusion.3 = bf16[16,148,512]{2,1,0:T(8,128)(2,1)S(1)} fusion(bf16[8,144,512]{2,1,0:T(8,128)(2,1)} %param.5, bf16[8,144,512]{2,1,0:T(8,128)(2,1)} %param.4), kind=kLoop, calls=%fused_computation.7 | loop fusion | flops 10911744 | bytes 4784128 | tf_op jit(solution)/shard_map/concatenate | solution.py:128
  9.9 3.4 %slice.116 = bf16[16,48,512]{2,1,0:T(8,128)(2,1)} slice(bf16[16,148,512]{2,1,0:T(8,128)(2,1)S(1)} %fusion.3), slice={[0:16:1], [3:145:3], [0:512:1]} | slice | bytes 1572864 | tf_op jit(solution)/shard_map/slice | solution.py:60
  13.2 3.2 %slice.114 = bf16[16,48,512]{2,1,0:T(8,128)(2,1)} slice(bf16[16,148,512]{2,1,0:T(8,128)(2,1)S(1)} %fusion.3), slice={[0:16:1], [2:144:3], [0:512:1]} | slice | bytes 1572864 | tf_op jit(solution)/shard_map/slice | solution.py:60
  16.5 3.3 %slice.112 = bf16[16,48,512]{2,1,0:T(8,128)(2,1)} slice(bf16[16,148,512]{2,1,0:T(8,128)(2,1)S(1)} %fusion.3), slice={[0:16:1], [1:143:3], [0:512:1]} | slice | bytes 1572864 | tf_op jit(solution)/shard_map/slice | solution.py:60
  19.7 1.2 slice.110
  20.9 3.5 %slice.118 = bf16[16,48,512]{2,1,0:T(8,128)(2,1)} slice(bf16[16,148,512]{2,1,0:T(8,128)(2,1)S(1)} %fusion.3), slice={[0:16:1], [4:146:3], [0:512:1]} | slice | bytes 1572864 | tf_op jit(solution)/shard_map/slice | solution.py:60
  24.4 1.5 fusion.68
  25.9 1.3 convolution_add_fusion.7
  27.6 0.7 copy-done.5
  29.4 24.9 %all_to_all.5 = bf16[4,16,48,256]{3,2,1,0:T(8,128)(2,1)S(1)} all-to-all(bf16[4,16,48,256]{3,2,1,0:T(8,128)(2,1)S(1)} %broadcast_in_dim.16), channel_id=1, replica_groups=mesh['dp_0'=4,'dp_1'=4,'dp_2'=2,'section'=4] {'section'}, dimensions={0} | all-to-all | bytes 3145728 | tf_op jit(solution)/shard_map/all_to_all | solution.py:16
  54.3 1.2 copy.16
  56.1 1.3 pad_slice_fusion
  57.5 0.9 copy-done
  61.5 0.8 fusion.76
  63.1 0.6 fusion.44
  63.8 0.6 fusion.47
  64.4 0.6 fusion.41
  65.0 0.6 fusion.50
  65.6 2.0 add_convert_fusion
  67.9 1.7 fusion.75
  69.7 2.2 %fusion.17 = bf16[1024,5,256]{2,0,1:T(8,128)(2,1)S(1)} fusion(bf16[16,48,256]{2,1,0:T(8,128)(2,1)S(1)} %get-tuple-element.29, bf16[16,48,1024]{2,1,0:T(8,128)(2,1)} %bitcast.237), kind=kOutput, calls=%fused_computation.41 | convolution fusion | flops 402915328 | bytes 2490368 | tf_op jit(solution)/shard_map/dot_general | solution.py:95
  71.8 0.6 fusion.15
  72.5 0.6 fusion.9
  73.1 0.6 fusion.13
  73.7 0.6 fusion.11
  74.4 3.6 %copy.19 = bf16[1024,5,256]{2,1,0:T(8,128)(2,1)} copy(bf16[1024,5,256]{2,0,1:T(8,128)(2,1)S(1)} %fusion.11) | data formatting | bytes 5242880 | tf_op jit(solution)/shard_map/stack | solution.py:99
  78.0 4.7 %convert_element_type.93 = bf16[32,40960]{1,0:T(8,128)(2,1)S(1)} reshape(bf16[1024,5,256]{2,1,0:T(8,128)(2,1)} %copy.19) | data formatting | bytes 5242880 | tf_op jit(solution)/shard_map/convert_element_type | solution.py:156
  82.7 11.3 %reduce-scatter.3.cloned.1.call-done = bf16[16,48,256]{2,1,0:T(8,128)(2,1)} async-done(((bf16[16,48,1024]{2,1,0:T(8,128)(2,1)}), bf16[16,48,256]{2,1,0:T(8,128)(2,1)}) %reduce-scatter.3.cloned.1.call-update) | async-done | bytes 393232 | tf_op jit(solution)/shard_map/reduce_scatter | solution.py:143
  94.0 1.5 fusion.37
  96.0 0.7 copy-done.12
  97.1 0.7 copy-done.10
  98.2 0.7 copy-done.6
  99.4 0.7 copy-done.8
  100.5 2.2 %copy.18 = bf16[512,5,256]{2,1,0:T(8,128)(2,1)} copy(bf16[512,5,256]{2,0,1:T(8,128)(2,1)S(1)} %fusion.24) | data formatting | bytes 2621440 | tf_op jit(solution)/shard_map/stack | solution.py:99
  102.7 3.5 %convert_element_type.92 = bf16[32,20480]{1,0:T(8,128)(2,1)} reshape(bf16[512,5,256]{2,1,0:T(8,128)(2,1)} %copy.18) | data formatting | bytes 2621440 | tf_op jit(solution)/shard_map/convert_element_type | solution.py:156
  106.2 3.4 %pad_maximum_fusion = bf16[32,61440]{1,0:T(8,128)(2,1)} fusion(bf16[32,40960]{1,0:T(8,128)(2,1)S(1)} %convert_element_type.93, bf16[32,20480]{1,0:T(8,128)(2,1)} %convert_element_type.92), kind=kLoop, calls=%fused_computation.5 | loop fusion | flops 7864320 | bytes 7864320 | tf_op jit(solution)/shard_map/concatenate | solution.py:45
  109.7 5.4 %reshape.124 = bf16[15360,128]{1,0:T(8,128)(2,1)} reshape(bf16[32,61440]{1,0:T(8,128)(2,1)} %pad_maximum_fusion) | data formatting | bytes 7864320 | tf_op jit(solution)/shard_map/reshape | solution.py:47
  115.1 0.6 copy-done.17
  116.3 1.4 dynamic-update-slice
  117.7 1.4 dynamic-update-slice.4
  119.7 10.6 %all-reduce.13 = (f32[4]{0:T(128)S(1)}, f32[4]{0:T(128)S(1)}) all-reduce(f32[4]{0:T(128)S(1)} %dynamic-update-slice.4, f32[4]{0:T(128)S(1)} %dynamic-update-slice), channel_id=1, replica_groups=mesh['dp_0'=4,'dp_1'=4,'dp_2'=2,'section'=4] {'dp_0'}, use_global_device_ids=true, to_apply=%add.7 | all-reduce | flops 8 | bytes 64
  130.3 0.6 reduce_sum.91
  130.9 0.6 reduce_sum.96
  131.5 1.4 dynamic-update-slice.1
  132.9 1.4 dynamic-update-slice.5
  134.9 10.5 %all-reduce.12 = (f32[4]{0:T(128)S(1)}, f32[4]{0:T(128)S(1)}) all-reduce(f32[4]{0:T(128)S(1)} %dynamic-update-slice.5, f32[4]{0:T(128)S(1)} %dynamic-update-slice.1), channel_id=1, replica_groups=mesh['dp_0'=4,'dp_1'=4,'dp_2'=2,'section'=4] {'dp_1'}, use_global_device_ids=true, to_apply=%add.8 | all-reduce | flops 8 | bytes 64
  145.4 0.6 reduce_sum.92
  146.0 0.6 reduce_sum.97
  146.6 1.4 dynamic-update-slice.2
  148.0 1.4 dynamic-update-slice.6
  150.0 2.4 %all-reduce.14 = (f32[2]{0:T(128)S(1)}, f32[2]{0:T(128)S(1)}) all-reduce(f32[2]{0:T(128)S(1)} %dynamic-update-slice.6, f32[2]{0:T(128)S(1)} %dynamic-update-slice.2), channel_id=1, replica_groups=mesh['dp_0'=4,'dp_1'=4,'dp_2'=2,'section'=4] {'dp_2'}, use_global_device_ids=true, to_apply=%add.9 | all-reduce | flops 4 | bytes 32
  152.4 0.6 reduce_sum.93
  153.1 0.6 reduce_sum.98
  153.7 1.4 dynamic-update-slice.3
  155.1 1.4 dynamic-update-slice.7
  156.5 9.0 %all-reduce.11 = (f32[4]{0:T(128)S(1)}, f32[4]{0:T(128)S(1)}) all-reduce(f32[4]{0:T(128)S(1)} %dynamic-update-slice.7, f32[4]{0:T(128)S(1)} %dynamic-update-slice.3), channel_id=1, replica_groups=mesh['dp_0'=4,'dp_1'=4,'dp_2'=2,'section'=4] {'section'}, use_global_device_ids=true, to_apply=%add.10 | all-reduce | flops 8 | bytes 64
  165.4 0.6 reduce_sum.94
  166.0 0.6 reduce_sum.99
  166.6 1.9 maximum_multiply_fusion
  168.5 28.3 %reduce-scatter.5.cloned.1.call-done = bf16[480,128]{1,0:T(8,128)(2,1)} async-done(((bf16[15360,128]{1,0:T(8,128)(2,1)}), bf16[480,128]{1,0:T(8,128)(2,1)}) %reduce-scatter.5.cloned.1.call-update) | async-done | bytes 122896 | tf_op jit(solution)/shard_map/reduce_scatter | solution.py:48
  196.9 0.8 slice_convert_fusion.1
  197.7 0.7 copy.20
  198.4 0.9 slice_convert_fusion
  199.3 0.7 copy.21
  (68 shorter events, 10.7 us)
Async XLA Ops:
  7.2 86.8 %reduce-scatter.3.cloned.1.call-start = ((), (), s32[]{:S(2)}) async-start(), calls=%async_computation.3 | async-start | bytes 1966080 | tf_op jit(solution)/shard_map/reduce_scatter | solution.py:143
  20.9 6.3 %copy-start.3 = (bf16[16,48,512]{2,1,0:T(8,128)(2,1)}, bf16[16,48,512]{2,1,0:T(8,128)(2,1)S(1)}, u32[]{:S(2)}) copy-start(bf16[16,48,512]{2,1,0:T(8,128)(2,1)S(1)} %slice.110) | copy-start | bytes 2359300
  24.4 1.5 copy-start.11
  24.4 2.8 %copy-start.9 = (bf16[16,48,512]{2,1,0:T(8,128)(2,1)S(1)}, bf16[16,48,512]{2,1,0:T(8,128)(2,1)}, u32[]{:S(2)}) copy-start(bf16[16,48,512]{2,1,0:T(8,128)(2,1)} %slice.114) | copy-start | bytes 2359300
  24.4 2.8 %copy-start.13 = (bf16[5,512,256]{2,1,0:T(8,128)(2,1)S(1)}, bf16[5,512,256]{2,1,0:T(8,128)(2,1)}, u32[]{:S(2)}) copy-start(bf16[5,512,256]{2,1,0:T(8,128)(2,1)} %param.6) | copy-start | bytes 3932164
  27.2 1.1 copy-start.5
  27.6 1.2 copy-start.7
  56.1 1.4 copy-start.1
  56.1 2.3 %copy-start = (bf16[5,1024,256]{2,1,0:T(8,128)(2,1)S(1)}, bf16[5,1024,256]{2,1,0:T(8,128)(2,1)}, u32[]{:S(2)}) copy-start(bf16[5,1024,256]{2,1,0:T(8,128)(2,1)} %param.7) | copy-start | bytes 7864324
  67.6 129.2 %reduce-scatter.5.cloned.1.call-start = ((), (), s32[]{:S(2)}) async-start(), calls=%async_computation.4 | async-start | bytes 4055040 | tf_op jit(solution)/shard_map/reduce_scatter | solution.py:48
  69.7 2.2 %copy-start.2 = (bf16[4,16,6,8,256]{4,3,0,2,1:T(8,128)(2,1)S(1)}, bf16[4,16,6,8,256]{4,3,0,2,1:T(8,128)(2,1)}, u32[]{:S(2)}) copy-start(bf16[4,16,6,8,256]{4,3,0,2,1:T(8,128)(2,1)} %copy-done.1) | copy-start | bytes 4718596
  94.0 1.5 copy-start.4
  95.5 1.1 copy-start.12
  96.7 1.1 copy-start.10
  97.8 1.1 copy-start.6
  99.0 1.1 copy-start.8
  115.1 0.7 copy-start.17
  115.1 4.0 %copy-start.16 = (u32[128]{0:T(128)S(1)}, u32[128]{0:T(128)}, u32[]{:S(2)}) copy-start(u32[128]{0:T(128)} %constant.40) | copy-start | bytes 1540
  115.1 19.3 %copy-start.15 = (u32[128]{0:T(128)S(1)}, u32[128]{0:T(128)}, u32[]{:S(2)}) copy-start(u32[128]{0:T(128)} %constant.45) | copy-start | bytes 1540
  115.1 34.3 %copy-start.14 = (u32[128]{0:T(128)S(1)}, u32[128]{0:T(128)}, u32[]{:S(2)}) copy-start(u32[128]{0:T(128)} %constant.50) | copy-start | bytes 1540
Sparse Core Ops, SparseCore 0:
  67.8 26.2 reduce-scatter.2
  115.2 81.5 reduce-scatter.4
